TPU v7x, 32 devices: a whole 2x2x4 slice. The times are simulated.
32 devices in a mesh: replica: 4 (over y, x), shard: 8 (over z, core).
Axes of the slice: x: 2, y: 2, z: 4, core: 2. Of those that a mesh axis runs over, the one named last changes fastest.
Arguments:
- tokens: bfloat16 [4096, 4096], P(('replica', 'shard')), parts along dimension 0, may hold values from -6 to 6
- queries: bfloat16 [4096, 2048], P(('replica', 'shard')), parts along dimension 0, may hold values from -48 to 48
- values: bfloat16 [4096, 512], P(('replica', 'shard')), parts along dimension 0, may hold values from -6 to 6
- out_grad: bfloat16 [4096, 2048], P(('replica', 'shard')), parts along dimension 0, may hold values from -6 to 6
- w_key: bfloat16 [16384, 512], P(('replica', 'shard')), parts along dimension 0, may hold values from -0.09375 to 0.09375
- norm_gain: bfloat16 [16384], P(('replica', 'shard')), parts along dimension 0, may hold values from 0.5 to 1.5
- key_momentum: float32 [16384, 512], P(('replica', 'shard')), parts along dimension 0, may hold values from -6 to 6
- gain_momentum: float32 [16384], P(('replica', 'shard')), parts along dimension 0, may hold values from -6 to 6
Outputs:
- attended: bfloat16 [4096, 2048], P(('replica', 'shard')), parts along dimension 0
- new_key_weight: bfloat16 [16384, 512], P(('replica', 'shard')), parts along dimension 0
- new_key_momentum: float32 [16384, 512], P(('replica', 'shard')), parts along dimension 0
- new_gain: bfloat16 [16384], P(('replica', 'shard')), parts along dimension 0
- new_gain_momentum: float32 [16384], P(('replica', 'shard')), parts along dimension 0
There are 4 independent parts, one for each index of `replica`. A program takes and returns all parts, laid end to end along the dimension named above; each array names one. Nothing has to cross between parts.
All inputs are finite; a program needn't handle non-finite values.
Results may differ from a plain program's by a relative error of at most 0.02.
Values may be sent and summed in bfloat16 or wider, within the bound.
No kernel may reach another device: no remote copies, remote signals or barrier semaphores. Data moves between devices by JAX's collectives and lax.ppermute only.
A program may use at most 128 MiB of HBM per device.

v0:
```python
import math
import jax
import jax.numpy as jnp
from jax import lax
from jax.sharding import PartitionSpec as P

HD = 128
epsilon = 1e-05
rope_base = 500000.0
inertia = 0.9
step_size = 0.01


def rotation_tables(positions, head_width):
    half_width = head_width // 2
    exponent = jnp.arange(half_width, dtype=jnp.float32) * (2.0 / head_width)
    frequency = jnp.exp(-math.log(rope_base) * exponent)
    angles = positions.astype(jnp.float32)[:, None] * frequency[None, :]
    return (jnp.cos(angles)[:, None, :], jnp.sin(angles)[:, None, :])


def rotate_keys(raw_rows, cosine, sine_table):
    first_half, second_half = jnp.split(raw_rows, 2, axis=-1)
    return jnp.concatenate(
        [
            first_half * cosine - second_half * sine_table,
            second_half * cosine + first_half * sine_table,
        ],
        axis=-1,
    )


def rotate_back(grad_rows, cosine, sine_table):
    first_half, second_half = jnp.split(grad_rows, 2, axis=-1)
    return jnp.concatenate(
        [
            first_half * cosine + second_half * sine_table,
            second_half * cosine - first_half * sine_table,
        ],
        axis=-1,
    )


def shards(tokens, queries, values, out_grad, w_key, norm_gain, key_momentum, gain_momentum):
    token_rows, model_width = tokens.shape
    key_width = w_key.shape[1]
    head_width = HD
    key_heads = key_width // head_width
    group_size = queries.shape[1] // key_width
    score_scale = head_width ** (-0.5)
    my_index = lax.axis_index("shard")
    first_token = my_index * token_rows
    last_token = first_token + token_rows - 1
    positions = first_token + jnp.arange(token_rows, dtype=jnp.int32)
    cosine, sine_table = rotation_tables(positions, head_width)
    inputs_float = tokens.astype(jnp.float32)
    inverse_rms = lax.rsqrt(jnp.mean(inputs_float * inputs_float, axis=1, keepdims=True) + epsilon)
    normalized = inputs_float * inverse_rms
    weight_rows = lax.all_gather(w_key, "shard", axis=0, tiled=True)
    gain_rows = lax.all_gather(norm_gain, "shard", axis=0, tiled=True)
    scaled = (normalized * gain_rows.astype(jnp.float32)[None, :]).astype(jnp.bfloat16)
    key_sum = jnp.dot(scaled, weight_rows, preferred_element_type=jnp.float32)
    key_local = rotate_keys(key_sum.reshape(token_rows, key_heads, head_width), cosine, sine_table)
    key_local = key_local.reshape(token_rows, key_width).astype(jnp.bfloat16)
    all_keys, all_values = (
        lax.all_gather(key_local, "shard", axis=0, tiled=True),
        lax.all_gather(values, "shard", axis=0, tiled=True),
    )
    total_tokens = all_keys.shape[0]
    query_heads = queries.reshape(token_rows, key_heads, group_size, head_width)
    grad_heads = out_grad.reshape(token_rows, key_heads, group_size, head_width)

    def block_scores(block_keys, block_begin):
        scores = (
            jnp.einsum(
                "tghd,sgd->ghts", query_heads, block_keys, preferred_element_type=jnp.float32
            )
            * score_scale
        )
        key_pos = block_begin + jnp.arange(block_keys.shape[0], dtype=jnp.int32)
        allowed = key_pos[None, :] <= positions[:, None]
        return jnp.where(allowed[None, None], scores, -jnp.inf)

    block_width = math.gcd(total_tokens, 512)
    block_total = total_tokens // block_width
    key_blocks = all_keys.reshape(block_total, block_width, key_heads, head_width)
    value_blocks = all_values.reshape(block_total, block_width, key_heads, head_width)
    block_starts = jnp.arange(block_total, dtype=jnp.int32) * block_width

    def max_pass(running, inputs):
        block_keys, block_begin = inputs

        def live_max():
            return jnp.maximum(running, jnp.max(block_scores(block_keys, block_begin), axis=-1))

        return (lax.cond(block_begin <= last_token, live_max, lambda: running), None)

    max_start = jnp.full((key_heads, group_size, token_rows), -jnp.inf, jnp.float32)
    row_max, unused = lax.scan(max_pass, max_start, (key_blocks, block_starts))

    def sum_pass(running, inputs):
        block_keys, block_values, block_begin = inputs

        def live_sum():
            denominator, numerator = running
            weights = jnp.exp(block_scores(block_keys, block_begin) - row_max[..., None])
            denominator = denominator + jnp.sum(weights, axis=-1)
            numerator = numerator + jnp.einsum(
                "ghts,sgd->tghd",
                weights.astype(jnp.bfloat16),
                block_values,
                preferred_element_type=jnp.float32,
            )
            return (denominator, numerator)

        return (lax.cond(block_begin <= last_token, live_sum, lambda: running), None)

    sum_start = (
        jnp.zeros((key_heads, group_size, token_rows), jnp.float32),
        jnp.zeros((token_rows, key_heads, group_size, head_width), jnp.float32),
    )
    (denominator, numerator), unused = lax.scan(
        sum_pass, sum_start, (key_blocks, value_blocks, block_starts)
    )
    attended_full = numerator / jnp.transpose(denominator, (2, 0, 1))[..., None]
    attended = attended_full.reshape(token_rows, key_width * group_size).astype(jnp.bfloat16)
    delta_rows = jnp.einsum("tghd,tghd->ght", grad_heads.astype(jnp.float32), attended_full)
    row_count = lax.axis_size("shard") * token_rows
    inner_width = math.gcd(row_count, 512)
    inner_total = row_count // inner_width

    def one_block(counter):
        begin_here = counter * inner_width

        def live_term():
            block_keys = lax.dynamic_slice_in_dim(all_keys, begin_here, inner_width, 0).reshape(
                inner_width, key_heads, head_width
            )
            block_values = lax.dynamic_slice_in_dim(all_values, begin_here, inner_width, 0).reshape(
                inner_width, key_heads, head_width
            )
            probs = (
                jnp.exp(block_scores(block_keys, begin_here) - row_max[..., None])
                / denominator[..., None]
            )
            prob_grad = jnp.einsum(
                "tghd,sgd->ghts", grad_heads, block_values, preferred_element_type=jnp.float32
            )
            score_grad = (probs * (prob_grad - delta_rows[..., None])).astype(jnp.bfloat16)
            return (
                jnp.einsum(
                    "ghts,tghd->sgd", score_grad, query_heads, preferred_element_type=jnp.float32
                )
                * score_scale
            )

        def empty_term():
            return jnp.zeros((inner_width, key_heads, head_width), jnp.float32)

        return lax.cond(begin_here <= last_token, live_term, empty_term)

    block_terms = lax.map(one_block, jnp.arange(inner_total, dtype=jnp.int32))
    key_grads = lax.psum_scatter(
        block_terms.reshape(row_count, key_width).astype(jnp.bfloat16),
        "shard",
        scatter_dimension=0,
        tiled=True,
    ).astype(jnp.float32)
    raw_grads = rotate_back(
        key_grads.reshape(token_rows, key_heads, head_width), cosine, sine_table
    )
    raw_grads = raw_grads.reshape(token_rows, key_width).astype(jnp.bfloat16)
    columns = lax.all_to_all(normalized, "shard", split_axis=1, concat_axis=0, tiled=True)
    normed_columns = (columns * norm_gain.astype(jnp.float32)[None, :]).astype(jnp.bfloat16)
    grad_block = lax.all_gather(raw_grads, "shard", axis=0, tiled=True)
    weight_sum = jnp.einsum(
        "td,tk->dk", normed_columns, grad_block, preferred_element_type=jnp.float32
    )
    normed_grad = jnp.einsum("tk,dk->td", grad_block, w_key, preferred_element_type=jnp.float32)
    gain_sum = jnp.sum(normed_grad * columns, axis=0)
    new_key_momentum = inertia * key_momentum + weight_sum
    new_key_weight = (w_key.astype(jnp.float32) - step_size * new_key_momentum).astype(jnp.bfloat16)
    new_gain_momentum = inertia * gain_momentum + gain_sum
    new_gain = (norm_gain.astype(jnp.float32) - step_size * new_gain_momentum).astype(jnp.bfloat16)
    return (attended, new_key_weight, new_key_momentum, new_gain, new_gain_momentum)


def solution(mesh):
    in_specs = (
        P(("replica", "shard"), None),
        P(("replica", "shard"), None),
        P(("replica", "shard"), None),
        P(("replica", "shard"), None),
        P(("replica", "shard"), None),
        P(("replica", "shard")),
        P(("replica", "shard"), None),
        P(("replica", "shard")),
    )
    out_specs = (
        P(("replica", "shard"), None),
        P(("replica", "shard"), None),
        P(("replica", "shard"), None),
        P(("replica", "shard")),
        P(("replica", "shard")),
    )
    return jax.shard_map(shards, mesh=mesh, in_specs=in_specs, out_specs=out_specs, check_vma=False)
```

profile of v0, /device:TPU:0, one launch (start us, length us, event | category | flops | bytes accessed | tf_op | source)
XLA Modules:
  0.0 247.0 jit_solution(13793263313454300019)
XLA Ops:
  7.2 0.7 all-gather.6.cloned.1.call-update
  7.9 1.7 copy.48
  9.7 0.7 reshape.223
  10.4 14.5 %all-gather = bf16[8,1,512]{2,1,0:T(2,128)(2,1)S(1)} all-gather(bf16[1,1,512]{2,1,0:T(2,128)(2,1)S(1)} %reshape.223), channel_id=1, replica_groups=mesh['replica'=4,'shard'=8] {'shard'}, dimensions={0}, use_global_device_ids=true | all-gather | bytes 9216 | tf_op jit(solution)/shard_map/all_gather | solution.py:60
  24.9 1.5 fusion.46
  26.7 32.5 %all-gather.6.cloned.1.call-done = bf16[4096,512]{1,0:T(8,128)(2,1)} async-done(((bf16[512,512]{1,0:T(8,128)(2,1)}), bf16[4096,512]{1,0:T(8,128)(2,1)}) %all-gather.6.cloned.1.call-update) | async-done | bytes 4194320 | tf_op jit(solution)/shard_map/all_gather | solution.py:59
  59.2 3.3 %fusion.49 = f32[128,512]{1,0:T(8,128)S(1)} fusion(bf16[4096,512]{1,0:T(8,128)(2,1)} %all-gather.6.cloned.1.call-done, f32[4096]{0:T(1024)S(1)} %bitcast.166, bf16[128,4096]{1,0:T(8,128)(2,1)} %param.20, f32[128]{0:T(128)S(1)} %add_rsqrt_fusion), kind=kOutput, calls=%fused_computation.64 | convolution fusion | flops 538968064 | bytes 5521920 | tf_op jit(solution)/shard_map/dot_general | solution.py:62
  63.1 0.8 copy.44
  65.0 1.0 copy.56
  66.0 18.1 %all-gather.10.cloned.1.call-done = bf16[1024,512]{0,1:T(8,128)(2,1)} async-done(((bf16[128,512]{0,1:T(8,128)(2,1)}), bf16[1024,512]{0,1:T(8,128)(2,1)}) %all-gather.10.cloned.1.call-update) | async-done | bytes 1048592 | tf_op jit(solution)/shard_map/all_gather | solution.py:67
  84.1 1.8 reshape.217
  85.9 2.0 copy.51
  87.9 21.0 %all-gather.8.cloned.1.call-done = bf16[1024,512]{0,1:T(8,128)(2,1)} async-done(((bf16[128,512]{0,1:T(8,128)(2,1)}), bf16[1024,512]{0,1:T(8,128)(2,1)}) %all-gather.8.cloned.1.call-update) | async-done | bytes 1048592 | tf_op jit(solution)/shard_map/all_gather | solution.py:66
  108.9 1.8 reshape.215
  110.8 0.9 copy.49
  111.7 4.1 %while.38 = (s32[]{:T(128)}, f32[4,4,128]{2,1,0:T(4,128)S(1)}, s32[2]{0:T(128)S(1)}, s32[]{:T(128)}, bf16[2,512,4,128]{3,1,2,0:T(8,128)(2,1)S(1)}, /*index=5*/bf...) while((s32[]{:T(128)}, f32[4,4,128]{2,1,0:T(4,128)S(1)}, s32[2]{0:T(128)S(1)}, s32[]{:T(128)}, ...), condition=%wide.region_5.6_spmd.clone, body=%wide.region_1.5_spmd.clone.sunk | while | flops 271647360 | bytes 1218747 | solution.py:99
  111.7 0.6 dynamic_slice.60
  113.0 1.6 conditional.9
  113.0 0.7 iota_add_fusion
  113.8 0.7 fusion.6
  115.8 1.0 copy-done.5
  116.9 7.1 %while.39 = (s32[]{:T(128)}, f32[4,4,128]{2,1,0:T(4,128)S(1)}, f32[128,4,4,128]{3,0,2,1:T(8,128)S(1)}, s32[2]{0:T(128)S(1)}, s32[]{:T(128)}, /*index=5*/bf16[2,5...) while((s32[]{:T(128)}, f32[4,4,128]{2,1,0:T(4,128)S(1)}, ...), condition=%wide.region_10.11_spmd.clone, body=%wide.region_6.10_spmd.clone.sunk | while | flops 545587840 | bytes 16505639 | solution.py:122
  118.2 4.6 %conditional.10 = ((f32[4,4,128]{2,1,0:T(4,128)S(1)}, f32[128,4,4,128]{3,0,2,1:T(8,128)S(1)})) conditional(s32[]{:T(128)} %convert_element_type.125, (f32[4,4,128]{2,1,0:T(4,128)S(1)}, f32[128,4,4,128]{3,0,2,1:T(8,128)S(1)}) %tuple.114, (s32[]{:T(128)}, s32[]{:T(128)}, bf16[2,512,4,128]{3,1,2,0:T(8,128)(2,1)}, s32[]{:T(128)}, ...), branch_computations={%region_7.7_spmd, %region_8.9_spmd} | conditional | flops 545587840 | bytes 16504896 | solution.py:116
  118.2 0.7 iota_add_fusion.1
  119.1 2.1 fusion.13
  121.2 1.5 fusion.23
  124.1 1.5 fusion.51
  125.5 1.6 copy.70
  127.3 12.9 %while.40 = (s32[]{:T(128)}, bf16[2,512,4,128]{3,1,2,0:T(8,128)(2,1)}, s32[2]{0:T(128)S(1)}, s32[]{:T(128)}, bf16[1024,512]{0,1:T(8,128)(2,1)}, /*index=5*/bf16[...) while((s32[]{:T(128)}, ...), condition=%wide.region_14.15_spmd.clone, body=%wide.region_11.14_spmd.clone.sunk | while | flops 813236864 | bytes 16939852 | solution.py:162
  128.5 8.5 %conditional.11 = (bf16[1,512,4,128]{3,1,2,0:T(8,128)(2,1)S(1)}) conditional(s32[]{:T(128)} %convert_element_type.126, () %tuple.117, (s32[]{:T(128)}, s32[]{:T(128)}, bf16[1024,512]{0,1:T(8,128)(2,1)}, bf16[128,4,4,128]{3,0,2,1:T(8,128)(2,1)S(1)}, f32[4,4,128]{2,1,0:T(4,128)S(1)}, /*index=5*/f32[4,4,128]{2,1,0:T(4,128)S(1)}, ...), branch_computations={%region_12.12_spmd, %region_13.13_spmd} | conditional | flops 813236864 | bytes 15890002 | solution.py:160
  128.6 1.6 constant_dynamic-slice_fusion
  130.2 2.7 %fusion.53 = f32[4,512,128,4]{2,1,3,0:T(8,128)} fusion(bf16[512,4,128,1]{0,2,3,1:T(8,128)(2,1)S(1)} %bitcast.154, bf16[128,4,4,128]{3,0,2,1:T(8,128)(2,1)S(1)} %get-tuple-element.277), kind=kOutput, calls=%fused_computation.87 | convolution fusion | flops 268435456 | bytes 5242880 | tf_op jit(solution)/shard_map/while/body/eval_jaxpr/cond/branch_1_fun/tghd,sgd->ghts/dot_general | solution.py:75
  133.1 4.0 %fusion.43 = bf16[1,512,4,128]{3,1,2,0:T(8,128)(2,1)S(1)} fusion(bf16[128,4,4,128]{3,0,2,1:T(8,128)(2,1)S(1)} %get-tuple-element.277, f32[4,512,128,4]{2,1,3,0:T(8,128)} %fusion.53, bf16[512,4,128,1]{0,2,3,1:T(8,128)(2,1)S(1)} %bitcast.155, bf16[128,4,4,128]{3,0,2,1:T(8,128)(2,1)S(1)} %copy-done.8, f32[4,4,128]{2,1,0:T(4,128)S(1)} %get-tuple-element.282, ...), kind=kOutput, calls=%fused_computation.45 | convolution fusion | flops 544735232 | bytes 6381568 | tf_op jit(solution)/shard_map/while/body/eval_jaxpr/cond/branch_1_fun/ghts,tghd->sgd/dot_general | solution.py:151
  137.1 0.9 constant_dynamic-update-slice_fusion.2
  139.3 0.8 constant_dynamic-update-slice_fusion.2
  140.1 2.1 copy.57
  142.3 1.2 copy.83
  143.7 1.6 copy.82
  145.3 18.3 %all-to-all-start = ((f32[128,8,512]{2,0,1:T(8,128)}), f32[128,8,512]{2,0,1:T(8,128)S(1)}, u32[]{:S(2)}, u32[]{:S(2)}) async-start(f32[128,8,512]{2,0,1:T(8,128)} %bitcast.156), calls=%async_computation | async-start | bytes 4194304 | tf_op jit(solution)/shard_map/all_to_all | solution.py:173
  163.8 32.9 %reduce-scatter.2.cloned.1.call-done = bf16[128,512]{1,0:T(8,128)(2,1)} async-done(((bf16[1024,512]{1,0:T(8,128)(2,1)}), bf16[128,512]{1,0:T(8,128)(2,1)}) %reduce-scatter.2.cloned.1.call-update) | async-done | bytes 131088 | tf_op jit(solution)/shard_map/reduce_scatter | solution.py:163
  196.7 1.0 reshape.222
  198.2 0.7 copy.84
  198.9 30.5 %all-to-all-done = f32[128,8,512]{2,0,1:T(8,128)S(1)} async-done(((f32[128,8,512]{2,0,1:T(8,128)}), f32[128,8,512]{2,0,1:T(8,128)S(1)}, u32[]{:S(2)}, u32[]{:S(2)}) %all-to-all-start) | async-done | bytes 2097184 | tf_op jit(solution)/shard_map/all_to_all | solution.py:173
  229.4 1.3 fusion.47
  230.7 1.2 copy.52
  231.9 2.2 convert_element_type.77
  234.2 2.0 fusion.48
  236.7 3.8 %subtract_convert_fusion = (bf16[512,512]{1,0:T(8,128)(2,1)}, f32[512,512]{1,0:T(8,128)}) fusion(bf16[512,512]{1,0:T(8,128)(2,1)S(1)} %copy-done.1, bf16[1024,512]{1,0:T(8,128)(2,1)} %fusion.47, bf16[1024,512]{1,0:T(8,128)(2,1)} %all-gather.12.cloned.1.call-done, f32[512,512]{1,0:T(8,128)} %param.26), kind=kOutput, calls=%fused_computation.67 | convolution fusion | flops 538443776 | bytes 5242880 | tf_op jit(solution)/shard_map/td,tk->dk/dot_general | solution.py:176
  (78 shorter events, 7.6 us)
Async XLA Ops:
  7.2 52.0 %all-gather.6.cloned.1.call-start = ((), (), s32[]{:S(2)}) async-start(), calls=%async_computation.2 | async-start | bytes 4718592 | tf_op jit(solution)/shard_map/all_gather | solution.py:59
  7.9 76.2 %all-gather.10.cloned.1.call-start = ((), (), s32[]{:S(2)}) async-start(), calls=%async_computation.4 | async-start | bytes 1179648 | tf_op jit(solution)/shard_map/all_gather | solution.py:67
  9.6 99.3 %all-gather.8.cloned.1.call-start = ((), (), s32[]{:S(2)}) async-start(), calls=%async_computation.3 | async-start | bytes 1179648 | tf_op jit(solution)/shard_map/all_gather | solution.py:66
  26.4 37.7 %copy-start.6 = (bf16[128,2048]{1,0:T(8,128)(2,1)S(1)}, bf16[128,2048]{1,0:T(8,128)(2,1)}, u32[]{:S(2)}) copy-start(bf16[128,2048]{1,0:T(8,128)(2,1)} %param.21) | copy-start | bytes 1572868
  59.2 5.5 %copy-start.7 = (bf16[128,2048]{1,0:T(8,128)(2,1)S(1)}, bf16[128,2048]{1,0:T(8,128)(2,1)}, u32[]{:S(2)}) copy-start(bf16[128,2048]{1,0:T(8,128)(2,1)} %param.23) | copy-start | bytes 1572868
  63.9 132.8 %reduce-scatter.2.cloned.1.call-start = ((), (), s32[]{:S(2)}) async-start(), calls=%async_computation.5 | async-start | bytes 1179648 | tf_op jit(solution)/shard_map/reduce_scatter | solution.py:163
  115.8 1.0 copy-start.5
  118.2 3.0 %copy-start.4 = (bf16[2,512,4,128]{3,1,2,0:T(8,128)(2,1)S(1)}, bf16[2,512,4,128]{3,1,2,0:T(8,128)(2,1)}, u32[]{:S(2)}) copy-start(bf16[2,512,4,128]{3,1,2,0:T(8,128)(2,1)} %get-tuple-element.260) | copy-start | bytes 3145732 | tf_op jit(solution)/shard_map/while/body/eval_jaxpr/cond
  124.1 3.2 %copy-start = (bf16[1024,512]{0,1:T(8,128)(2,1)S(1)}, bf16[1024,512]{0,1:T(8,128)(2,1)}, u32[]{:S(2)}) copy-start(bf16[1024,512]{0,1:T(8,128)(2,1)} %all-gather.10.cloned.1.call-done) | copy-start | bytes 3145732
  128.6 4.5 %copy-start.8 = (bf16[128,4,4,128]{3,0,2,1:T(8,128)(2,1)S(1)}, bf16[128,4,4,128]{3,0,2,1:T(8,128)(2,1)}, u32[]{:S(2)}) copy-start(bf16[128,4,4,128]{3,0,2,1:T(8,128)(2,1)} %get-tuple-element.281) | copy-start | bytes 1572868 | tf_op jit(solution)/shard_map/while/body/eval_jaxpr/cond
  140.1 3.3 %copy-start.2 = (bf16[128,4096]{1,0:T(8,128)(2,1)S(1)}, bf16[128,4096]{1,0:T(8,128)(2,1)}, u32[]{:S(2)}) copy-start(bf16[128,4096]{1,0:T(8,128)(2,1)} %param.20) | copy-start | bytes 3145732
  145.3 53.7 %copy-start.9 = (bf16[512]{0:T(512)(128)(2,1)S(1)}, bf16[512]{0:T(512)(128)(2,1)}, u32[]{:S(2)}) copy-start(bf16[512]{0:T(512)(128)(2,1)} %param.25) | copy-start | bytes 3076
  145.3 85.5 %copy-start.3 = (bf16[128,4,4,128]{3,0,2,1:T(8,128)(2,1)S(1)}, bf16[128,4,4,128]{3,0,2,1:T(8,128)(2,1)}, u32[]{:S(2)}) copy-start(bf16[128,4,4,128]{3,0,2,1:T(8,128)(2,1)} %get-tuple-element.556) | copy-start | bytes 1572868
  145.3 84.2 %all-to-all-start = ((f32[128,8,512]{2,0,1:T(8,128)}), f32[128,8,512]{2,0,1:T(8,128)S(1)}, u32[]{:S(2)}, u32[]{:S(2)}) async-start(f32[128,8,512]{2,0,1:T(8,128)} %bitcast.156), calls=%async_computation | async-start | bytes 4194304 | tf_op jit(solution)/shard_map/all_to_all | solution.py:173
  163.5 70.6 %copy-start.1 = (bf16[512,512]{1,0:T(8,128)(2,1)S(1)}, bf16[512,512]{1,0:T(8,128)(2,1)}, u32[]{:S(2)}) copy-start(bf16[512,512]{1,0:T(8,128)(2,1)} %param.24) | copy-start | bytes 1572868
  163.5 70.6 %all-gather.12.cloned.1.call-start = ((), (), s32[]{:S(2)}) async-start(), calls=%async_computation.6 | async-start | bytes 1179648 | tf_op jit(solution)/shard_map/all_gather | solution.py:175
  198.9 37.2 %copy-start.10 = (f32[512]{0:T(512)S(1)}, f32[512]{0:T(512)}, u32[]{:S(2)}) copy-start(f32[512]{0:T(512)} %param.27) | copy-start | bytes 6148
Sparse Core Ops, SparseCore 0:
  9.6 49.5 all-gather.5
  61.4 22.6 all-gather.9
  86.2 22.6 all-gather.7
  143.5 53.1 reduce-scatter.1
  199.0 27.4 all-gather.11
where the time goes:
time: 248 us; the launch traced here: 247 us
  waiting for transfers between devices  136 us (55%)
  local copies, waits for them, and re-layouts  31.2 us (13%)
  matrix products  20.1 us (8%)
  starting transfers between devices  18.9 us (8%)
  blocking collectives  14.5 us (6%)
  between operations  14.1 us (6%)
  other arithmetic  8.36 us (3%)
  loops' own time  4.27 us (2%)
    reduce_scatter x1, waiting for transfers between devices, shards(): lax.psum_scatter(block_terms.reshape(row_count, key_width).astype(jnp.bfl...  32.9 us
    all_gather x1, waiting for transfers between devices, shards(): weight_rows = lax.all_gather(w_key, 'shard', axis=0, tiled=True)  32.5 us
    all_to_all x1, waiting for transfers between devices, shards(): lax.all_to_all(normalized, 'shard', split_axis=1, concat_axis=0, tiled=True)  30.5 us
    all_gather x1, waiting for transfers between devices, shards(): lax.all_gather(key_local, 'shard', axis=0, tiled=True)  21 us
    all_to_all x1, starting transfers between devices, shards(): lax.all_to_all(normalized, 'shard', split_axis=1, concat_axis=0, tiled=True)  18.3 us
    all_gather x1, waiting for transfers between devices, shards(): lax.all_gather(values, 'shard', axis=0, tiled=True)  18.1 us
    all_gather x1, blocking collectives, shards(): gain_rows = lax.all_gather(norm_gain, 'shard', axis=0, tiled=True)  14.5 us
    unnamed x29, local copies, waits for them, and re-layouts  11.5 us
  transfers between devices with their start and end apart: 6, of which 5 were waited for; matrix products, arithmetic and copies ran while one was open for 9% of the time, Pallas kernels for 0%

commit v1 on v0

--- a/solution.py
+++ b/solution.py
@@ -56,7 +56,14 @@
     inputs_float = tokens.astype(jnp.float32)
     inverse_rms = lax.rsqrt(jnp.mean(inputs_float * inputs_float, axis=1, keepdims=True) + epsilon)
     normalized = inputs_float * inverse_rms
-    weight_rows = lax.all_gather(w_key, "shard", axis=0, tiled=True)
+    ring = [w_key]
+    for hop in range(7):
+        ring.append(lax.ppermute(ring[-1], "shard", [(dev, (dev + 1) % 8) for dev in range(8)]))
+    weight_rows = jnp.roll(
+        jnp.concatenate(ring[::-1], axis=0),
+        (lax.axis_index("shard") + 1) * ring[0].shape[0],
+        axis=0,
+    )
     gain_rows = lax.all_gather(norm_gain, "shard", axis=0, tiled=True)
     scaled = (normalized * gain_rows.astype(jnp.float32)[None, :]).astype(jnp.bfloat16)
     key_sum = jnp.dot(scaled, weight_rows, preferred_element_type=jnp.float32)

time: 248 us -> 267 us (1.077)
  waiting for transfers between devices: 136 us -> 145 us
  local copies, waits for them, and re-layouts: 31.2 us -> 35.2 us
  starting transfers between devices: 18.9 us -> 22.5 us
    ppermute x0 -> x7, waiting for transfers between devices: none -> 65.1 us  [shards(): lax.ppermute(ring[-1], 'shard', [(dev, (dev + 1) % 8) for dev in range(8)])]
    all_gather x1 -> x0, waiting for transfers between devices: 32.5 us -> none  [shards(): weight_rows = lax.all_gather(w_key, 'shard', axis=0, tiled=True)]
    all_gather x1, waiting for transfers between devices: 18.1 us -> 0.01 us  [shards(): lax.all_gather(values, 'shard', axis=0, tiled=True)]
    all_gather x1, waiting for transfers between devices: 21 us -> 16.2 us  [shards(): lax.all_gather(key_local, 'shard', axis=0, tiled=True)]
    unnamed x29 -> x44, local copies, waits for them, and re-layouts: 11.5 us -> 15.4 us
    all_to_all x1, starting transfers between devices: 18.3 us -> 21.2 us  [shards(): lax.all_to_all(normalized, 'shard', split_axis=1, concat_axis=0, tiled=True)]
  transfers between devices with their start and end apart: 6 -> 12, of which waited for: 5 -> 9; matrix products, arithmetic and copies ran while one was open for 9% -> 9% of each run, Pallas kernels for 0% -> 0%
where the time goes in v1:
time: 267 us; the launch traced here: 266 us
  waiting for transfers between devices  145 us (54%)
  local copies, waits for them, and re-layouts  35.2 us (13%)
  starting transfers between devices  22.5 us (8%)
  matrix products  20.8 us (8%)
  between operations  14.2 us (5%)
  blocking collectives  13.4 us (5%)
  other arithmetic  10.8 us (4%)
  loops' own time  4.19 us (2%)
    ppermute x7, waiting for transfers between devices, shards(): lax.ppermute(ring[-1], 'shard', [(dev, (dev + 1) % 8) for dev in range(8)])  65.1 us
    reduce_scatter x1, waiting for transfers between devices, shards(): lax.psum_scatter(block_terms.reshape(row_count, key_width).astype(jnp.bfl...  32.8 us
    all_to_all x1, waiting for transfers between devices, shards(): lax.all_to_all(normalized, 'shard', split_axis=1, concat_axis=0, tiled=True)  30.7 us
    all_to_all x1, starting transfers between devices, shards(): lax.all_to_all(normalized, 'shard', split_axis=1, concat_axis=0, tiled=True)  21.2 us
    all_gather x1, waiting for transfers between devices, shards(): lax.all_gather(key_local, 'shard', axis=0, tiled=True)  16.2 us
    unnamed x44, local copies, waits for them, and re-layouts  15.4 us
    all_gather x1, blocking collectives, shards(): gain_rows = lax.all_gather(norm_gain, 'shard', axis=0, tiled=True)  13.4 us
    dot_general x3, matrix products, block_scores(): jnp.einsum('tghd,sgd->ghts', query_heads, block_keys, preferred_element_t...  6.61 us
  transfers between devices with their start and end apart: 12, of which 9 were waited for; matrix products, arithmetic and copies ran while one was open for 9% of the time, Pallas kernels for 0%

profile of v1, /device:TPU:0, one launch (start us, length us, event | category | flops | bytes accessed | tf_op | source)
XLA Modules:
  0.0 266.0 jit_solution(5956593594497637627)
XLA Ops:
  7.8 11.1 %collective-permute-done = bf16[512,512]{1,0:T(8,128)(2,1)S(1)} collective-permute-done((bf16[512,512]{1,0:T(8,128)(2,1)}, bf16[512,512]{1,0:T(8,128)(2,1)S(1)}, u32[]{:S(2)}, u32[]{:S(2)}) %collective-permute-start) | collective-permute-done | bytes 524320 | tf_op jit(solution)/shard_map/ppermute | solution.py:61
  18.9 10.4 %collective-permute-done.1 = bf16[512,512]{1,0:T(8,128)(2,1)S(1)} collective-permute-done((bf16[512,512]{1,0:T(8,128)(2,1)S(1)}, bf16[512,512]{1,0:T(8,128)(2,1)S(1)}, u32[]{:S(2)}, u32[]{:S(2)}) %collective-permute-start.1) | collective-permute-done | bytes 524320 | tf_op jit(solution)/shard_map/ppermute | solution.py:61
  29.3 10.4 %collective-permute-done.2 = bf16[512,512]{1,0:T(8,128)(2,1)S(1)} collective-permute-done((bf16[512,512]{1,0:T(8,128)(2,1)S(1)}, bf16[512,512]{1,0:T(8,128)(2,1)S(1)}, u32[]{:S(2)}, u32[]{:S(2)}) %collective-permute-start.2) | collective-permute-done | bytes 524320 | tf_op jit(solution)/shard_map/ppermute | solution.py:61
  39.7 10.4 %collective-permute-done.3 = bf16[512,512]{1,0:T(8,128)(2,1)S(1)} collective-permute-done((bf16[512,512]{1,0:T(8,128)(2,1)S(1)}, bf16[512,512]{1,0:T(8,128)(2,1)S(1)}, u32[]{:S(2)}, u32[]{:S(2)}) %collective-permute-start.3) | collective-permute-done | bytes 524320 | tf_op jit(solution)/shard_map/ppermute | solution.py:61
  50.1 10.4 %collective-permute-done.4 = bf16[512,512]{1,0:T(8,128)(2,1)S(1)} collective-permute-done((bf16[512,512]{1,0:T(8,128)(2,1)S(1)}, bf16[512,512]{1,0:T(8,128)(2,1)S(1)}, u32[]{:S(2)}, u32[]{:S(2)}) %collective-permute-start.4) | collective-permute-done | bytes 524320 | tf_op jit(solution)/shard_map/ppermute | solution.py:61
  60.5 1.7 copy.48
  62.9 13.4 %all-gather = bf16[8,1,512]{2,1,0:T(2,128)(2,1)S(1)} all-gather(bf16[1,1,512]{2,1,0:T(2,128)(2,1)S(1)} %reshape.223), channel_id=1, replica_groups=mesh['replica'=4,'shard'=8] {'shard'}, dimensions={0}, use_global_device_ids=true | all-gather | bytes 9216 | tf_op jit(solution)/shard_map/all_gather | solution.py:67
  76.4 1.6 fusion.48
  78.5 12.4 %collective-permute-done.6 = bf16[512,512]{1,0:T(8,128)(2,1)S(1)} collective-permute-done((bf16[512,512]{1,0:T(8,128)(2,1)}, bf16[512,512]{1,0:T(8,128)(2,1)S(1)}, u32[]{:S(2)}, u32[]{:S(2)}) %collective-permute-start.6) | collective-permute-done | bytes 524320 | tf_op jit(solution)/shard_map/ppermute | solution.py:61
  91.0 1.1 constant_dynamic-update-slice_fusion.15
  92.4 1.2 constant_dynamic-update-slice_fusion.7
  95.2 0.8 copy.44
  97.1 1.0 copy.56
  98.1 1.8 reshape.217
  100.0 2.1 copy.51
  102.0 16.2 %all-gather.5.cloned.1.call-done = bf16[1024,512]{0,1:T(8,128)(2,1)} async-done(((bf16[128,512]{0,1:T(8,128)(2,1)}), bf16[1024,512]{0,1:T(8,128)(2,1)}) %all-gather.5.cloned.1.call-update) | async-done | bytes 1048592 | tf_op jit(solution)/shard_map/all_gather | solution.py:73
  118.2 1.8 reshape.215
  120.1 2.1 copy.49
  122.1 5.1 %while.38 = (s32[]{:T(128)}, f32[4,4,128]{2,1,0:T(4,128)S(1)}, s32[2]{0:T(128)S(1)}, s32[]{:T(128)}, bf16[2,512,4,128]{3,1,2,0:T(8,128)(2,1)}, /*index=5*/bf16[128,4,4,128]{3,0,2,1:T(8,128)(2,1)S(1)}, s32[]{:T(128)}, s32[]{:T(128)}) while((s32[]{:T(128)}, f32[4,4,128]{2,1,0:T(4,128)S(1)}, s32[2]{0:T(128)S(1)}, s32[]{:T(128)}, ...), condition=%wide.region_5.6_spmd.clone, body=%wide.region_1.5_spmd.clone.sunk | while | flops 271647360 | bytes 1219255 | solution.py:106
  123.4 2.6 conditional.9
  124.2 1.8 fusion.6
  127.3 1.1 broadcast_in_dim.78
  128.4 8.9 %while.39 = (s32[]{:T(128)}, f32[4,4,128]{2,1,0:T(4,128)S(1)}, f32[128,4,4,128]{3,0,2,1:T(8,128)}, s32[2]{0:T(128)S(1)}, s32[]{:T(128)}, /*index=5*/bf16[2,512,4...) while((s32[]{:T(128)}, f32[4,4,128]{2,1,0:T(4,128)S(1)}, ...), condition=%wide.region_10.11_spmd.clone, body=%wide.region_6.10_spmd.clone.sunk | while | flops 545587840 | bytes 12311307 | solution.py:129
  129.6 6.4 %conditional.10 = ((f32[4,4,128]{2,1,0:T(4,128)S(1)}, f32[128,4,4,128]{3,0,2,1:T(8,128)})) conditional(s32[]{:T(128)} %convert_element_type.125, (f32[4,4,128]{2,1,0:T(4,128)S(1)}, f32[128,4,4,128]{3,0,2,1:T(8,128)}) %tuple.114, (s32[]{:T(128)}, s32[]{:T(128)}, bf16[2,512,4,128]{3,1,2,0:T(8,128)(2,1)}, s32[]{:T(128)}, ...), branch_computations={%region_7.7_spmd, %region_8.9_spmd} | conditional | flops 545587840 | bytes 12310564 | solution.py:123
  130.4 2.1 fusion.13
  132.6 3.5 %fusion.23 = f32[128,4,4,128]{3,0,2,1:T(8,128)} fusion(f32[128,4,4,128]{3,0,2,1:T(8,128)} %get-tuple-element.259, f32[4,512,128,4]{2,1,3,0:T(8,128)S(1)} %get-tuple-element.552, f32[4,4,128]{2,1,0:T(4,128)S(1)} %get-tuple-element.258, pred[128,512]{0,1:T(8,128)(4,1)S(1)} %broadcast_compare_fusion.1, bf16[2,512,4,128]{3,1,2,0:T(8,128)(2,1)S(1)} %get-tuple-element.260, ...), kind=kOutput, calls=%fused_computation.22 | convolution fusion | flops 272891904 | bytes 6889476 | tf_op jit(solution)/shard_map/while/body/eval_jaxpr/cond/branch_1_fun/ghts,sgd->tghd/dot_general | solution.py:115
  137.3 2.8 %fusion.52 = (f32[4,4,128,128]{3,2,1,0:T(8,128)}, bf16[128,4,4,128]{3,0,2,1:T(8,128)(2,1)}) fusion(f32[128,4,4,128]{3,0,2,1:T(8,128)} %get-tuple-element.306, f32[128,4,4]{0,2,1:T(4,128)S(1)} %bitcast.164), kind=kLoop, calls=%fused_computation.71 | loop fusion | flops 524288 | bytes 2629632
  140.1 2.5 copy.70
  142.6 1.4 multiply_reduce_fusion
  144.0 12.9 %while.40 = (s32[]{:T(128)}, bf16[2,512,4,128]{3,1,2,0:T(8,128)(2,1)}, s32[2]{0:T(128)S(1)}, s32[]{:T(128)}, bf16[1024,512]{0,1:T(8,128)(2,1)}, /*index=5*/bf16[...) while((s32[]{:T(128)}, ...), condition=%wide.region_14.15_spmd.clone, body=%wide.region_11.14_spmd.clone.sunk | while | flops 813236864 | bytes 14842673 | solution.py:169
  145.3 8.6 %conditional.11 = (bf16[1,512,4,128]{3,1,2,0:T(8,128)(2,1)S(1)}) conditional(s32[]{:T(128)} %convert_element_type.126, () %tuple.117, (s32[]{:T(128)}, s32[]{:T(128)}, bf16[1024,512]{0,1:T(8,128)(2,1)}, bf16[128,4,4,128]{3,0,2,1:T(8,128)(2,1)S(1)}, f32[4,4,128]{2,1,0:T(4,128)S(1)}, /*index=5*/f32[4,4,128]{2,1,0:T(4,128)S(1)}, ...), branch_computations={%region_12.12_spmd, %region_13.13_spmd} | conditional | flops 813236864 | bytes 13792822 | solution.py:167
  145.3 1.6 constant_dynamic-slice_fusion
  146.9 2.7 %fusion.55 = f32[4,512,128,4]{2,1,3,0:T(8,128)} fusion(bf16[512,4,128,1]{0,2,3,1:T(8,128)(2,1)S(1)} %bitcast.153, bf16[128,4,4,128]{3,0,2,1:T(8,128)(2,1)S(1)} %get-tuple-element.277), kind=kOutput, calls=%fused_computation.105 | convolution fusion | flops 268435456 | bytes 5242880 | tf_op jit(solution)/shard_map/while/body/eval_jaxpr/cond/branch_1_fun/tghd,sgd->ghts/dot_general | solution.py:82
  149.7 4.2 %fusion.43 = bf16[1,512,4,128]{3,1,2,0:T(8,128)(2,1)S(1)} fusion(bf16[128,4,4,128]{3,0,2,1:T(8,128)(2,1)S(1)} %get-tuple-element.277, f32[4,512,128,4]{2,1,3,0:T(8,128)} %fusion.55, bf16[512,4,128,1]{0,2,3,1:T(8,128)(2,1)S(1)} %bitcast.154, bf16[128,4,4,128]{3,0,2,1:T(8,128)(2,1)} %get-tuple-element.281, f32[4,4,128]{2,1,0:T(4,128)S(1)} %get-tuple-element.282, ...), kind=kOutput, calls=%fused_computation.45 | convolution fusion | flops 544735232 | bytes 6381568 | tf_op jit(solution)/shard_map/while/body/eval_jaxpr/cond/branch_1_fun/ghts,tghd->sgd/dot_general | solution.py:158
  153.9 0.8 constant_dynamic-update-slice_fusion.18
  156.1 0.9 constant_dynamic-update-slice_fusion.18
  156.9 2.1 copy.57
  159.1 1.2 copy.83
  160.5 1.6 copy.82
  162.1 21.2 %all-to-all-start = ((f32[128,8,512]{2,0,1:T(8,128)}), f32[128,8,512]{2,0,1:T(8,128)S(1)}, u32[]{:S(2)}, u32[]{:S(2)}) async-start(f32[128,8,512]{2,0,1:T(8,128)} %bitcast.155), calls=%async_computation | async-start | bytes 4194304 | tf_op jit(solution)/shard_map/all_to_all | solution.py:180
  183.6 32.8 %reduce-scatter.2.cloned.1.call-done = bf16[128,512]{1,0:T(8,128)(2,1)} async-done(((bf16[1024,512]{1,0:T(8,128)(2,1)}), bf16[128,512]{1,0:T(8,128)(2,1)}) %reduce-scatter.2.cloned.1.call-update) | async-done | bytes 131088 | tf_op jit(solution)/shard_map/reduce_scatter | solution.py:170
  216.3 1.0 reshape.222
  218.5 30.7 %all-to-all-done = f32[128,8,512]{2,0,1:T(8,128)S(1)} async-done(((f32[128,8,512]{2,0,1:T(8,128)}), f32[128,8,512]{2,0,1:T(8,128)S(1)}, u32[]{:S(2)}, u32[]{:S(2)}) %all-to-all-start) | async-done | bytes 2097184 | tf_op jit(solution)/shard_map/all_to_all | solution.py:180
  249.2 1.3 fusion.49
  250.5 1.4 copy.52
  251.9 1.2 convert_element_type.77
  253.1 2.0 fusion.50
  255.7 3.8 %subtract_convert_fusion = (bf16[512,512]{1,0:T(8,128)(2,1)}, f32[512,512]{1,0:T(8,128)}) fusion(bf16[512,512]{1,0:T(8,128)(2,1)S(1)} %copy-done.1, bf16[1024,512]{1,0:T(8,128)(2,1)} %fusion.49, bf16[1024,512]{1,0:T(8,128)(2,1)} %all-gather.9.cloned.1.call-done, f32[512,512]{1,0:T(8,128)} %param.26), kind=kOutput, calls=%fused_computation.68 | convolution fusion | flops 538443776 | bytes 5242880 | tf_op jit(solution)/shard_map/td,tk->dk/dot_general | solution.py:183
  (101 shorter events, 12.6 us)
Async XLA Ops:
  7.2 90.9 %all-gather.7.cloned.1.call-start = ((), (), s32[]{:S(2)}) async-start(), calls=%async_computation.3 | async-start | bytes 1179648 | tf_op jit(solution)/shard_map/all_gather | solution.py:74
  7.2 11.6 %collective-permute-start = (bf16[512,512]{1,0:T(8,128)(2,1)}, bf16[512,512]{1,0:T(8,128)(2,1)S(1)}, u32[]{:S(2)}, u32[]{:S(2)}) collective-permute-start(bf16[512,512]{1,0:T(8,128)(2,1)} %param.24), channel_id=1, source_target_pairs={{0,1},{1,2},{2,3},{3,4},{4,5},{5,6},{6,7},{7,0},{8,9},{9,10},{10,1... | collective-permute-start | bytes 1572872 | tf_op jit(solution)/shard_map/ppermute | solution.py:61
  18.9 10.4 %collective-permute-start.1 = (bf16[512,512]{1,0:T(8,128)(2,1)S(1)}, bf16[512,512]{1,0:T(8,128)(2,1)S(1)}, u32[]{:S(2)}, u32[]{:S(2)}) collective-permute-start(bf16[512,512]{1,0:T(8,128)(2,1)S(1)} %collective-permute-done), channel_id=1, source_target_pairs={{0,1},{1,2},{2,3},{3,4},{4,5},{5,6},{6,7},{7,0},{8,9},{9,10},{10,1... | collective-permute-start | bytes 1572872 | tf_op jit(solution)/shard_map/ppermute | solution.py:61
  29.3 10.4 %collective-permute-start.2 = (bf16[512,512]{1,0:T(8,128)(2,1)S(1)}, bf16[512,512]{1,0:T(8,128)(2,1)S(1)}, u32[]{:S(2)}, u32[]{:S(2)}) collective-permute-start(bf16[512,512]{1,0:T(8,128)(2,1)S(1)} %collective-permute-done.1), channel_id=1, source_target_pairs={{0,1},{1,2},{2,3},{3,4},{4,5},{5,6},{6,7},{7,0},{8,9},{9,10},{10,1... | collective-permute-start | bytes 1572872 | tf_op jit(solution)/shard_map/ppermute | solution.py:61
  39.7 10.4 %collective-permute-start.3 = (bf16[512,512]{1,0:T(8,128)(2,1)S(1)}, bf16[512,512]{1,0:T(8,128)(2,1)S(1)}, u32[]{:S(2)}, u32[]{:S(2)}) collective-permute-start(bf16[512,512]{1,0:T(8,128)(2,1)S(1)} %collective-permute-done.2), channel_id=1, source_target_pairs={{0,1},{1,2},{2,3},{3,4},{4,5},{5,6},{6,7},{7,0},{8,9},{9,10},{10,1... | collective-permute-start | bytes 1572872 | tf_op jit(solution)/shard_map/ppermute | solution.py:61
  50.1 10.4 %collective-permute-start.4 = (bf16[512,512]{1,0:T(8,128)(2,1)S(1)}, bf16[512,512]{1,0:T(8,128)(2,1)S(1)}, u32[]{:S(2)}, u32[]{:S(2)}) collective-permute-start(bf16[512,512]{1,0:T(8,128)(2,1)S(1)} %collective-permute-done.3), channel_id=1, source_target_pairs={{0,1},{1,2},{2,3},{3,4},{4,5},{5,6},{6,7},{7,0},{8,9},{9,10},{10,1... | collective-permute-start | bytes 1572872 | tf_op jit(solution)/shard_map/ppermute | solution.py:61
  60.5 17.5 %collective-permute-start.5 = (bf16[512,512]{1,0:T(8,128)(2,1)S(1)}, bf16[512,512]{1,0:T(8,128)(2,1)}, u32[]{:S(2)}, u32[]{:S(2)}) collective-permute-start(bf16[512,512]{1,0:T(8,128)(2,1)S(1)} %collective-permute-done.4), channel_id=1, source_target_pairs={{0,1},{1,2},{2,3},{3,4},{4,5},{5,6},{6,7},{7,0},{8,9},{9,10},{10,1... | collective-permute-start | bytes 1572872 | tf_op jit(solution)/shard_map/ppermute | solution.py:61
  62.2 56.1 %all-gather.5.cloned.1.call-start = ((), (), s32[]{:S(2)}) async-start(), calls=%async_computation.2 | async-start | bytes 1179648 | tf_op jit(solution)/shard_map/all_gather | solution.py:73
  76.4 15.9 %copy-start.1 = (bf16[512,512]{1,0:T(8,128)(2,1)S(1)}, bf16[512,512]{1,0:T(8,128)(2,1)}, u32[]{:S(2)}) copy-start(bf16[512,512]{1,0:T(8,128)(2,1)} %param.24) | copy-start | bytes 1572868
  78.0 13.0 %collective-permute-start.6 = (bf16[512,512]{1,0:T(8,128)(2,1)}, bf16[512,512]{1,0:T(8,128)(2,1)S(1)}, u32[]{:S(2)}, u32[]{:S(2)}) collective-permute-start(bf16[512,512]{1,0:T(8,128)(2,1)} %collective-permute-done.5), channel_id=1, source_target_pairs={{0,1},{1,2},{2,3},{3,4},{4,5},{5,6},{6,7},{7,0},{8,9},{9,10},{10,1... | collective-permute-start | bytes 1572872 | tf_op jit(solution)/shard_map/ppermute | solution.py:61
  92.3 1.5 copy-start.2
  93.8 2.4 copy-start.5
  93.8 3.0 %copy-start.6 = (bf16[128,2048]{1,0:T(8,128)(2,1)S(1)}, bf16[128,2048]{1,0:T(8,128)(2,1)}, u32[]{:S(2)}) copy-start(bf16[128,2048]{1,0:T(8,128)(2,1)} %param.23) | copy-start | bytes 1572868
  96.0 120.3 %reduce-scatter.2.cloned.1.call-start = ((), (), s32[]{:S(2)}) async-start(), calls=%async_computation.4 | async-start | bytes 1179648 | tf_op jit(solution)/shard_map/reduce_scatter | solution.py:170
  122.1 6.2 %copy-start.4 = (bf16[2,512,4,128]{3,1,2,0:T(8,128)(2,1)S(1)}, bf16[2,512,4,128]{3,1,2,0:T(8,128)(2,1)}, u32[]{:S(2)}) copy-start(bf16[2,512,4,128]{3,1,2,0:T(8,128)(2,1)} %copy.51) | copy-start | bytes 3145732
  137.3 6.7 %copy-start = (bf16[1024,512]{0,1:T(8,128)(2,1)S(1)}, bf16[1024,512]{0,1:T(8,128)(2,1)}, u32[]{:S(2)}) copy-start(bf16[1024,512]{0,1:T(8,128)(2,1)} %all-gather.7.cloned.1.call-done) | copy-start | bytes 3145732
  156.9 3.3 %copy-start.3 = (bf16[128,4096]{1,0:T(8,128)(2,1)S(1)}, bf16[128,4096]{1,0:T(8,128)(2,1)}, u32[]{:S(2)}) copy-start(bf16[128,4096]{1,0:T(8,128)(2,1)} %param.20) | copy-start | bytes 3145732
  162.1 56.4 %copy-start.7 = (bf16[512]{0:T(512)(128)(2,1)S(1)}, bf16[512]{0:T(512)(128)(2,1)}, u32[]{:S(2)}) copy-start(bf16[512]{0:T(512)(128)(2,1)} %param.25) | copy-start | bytes 3076
  162.1 87.1 %all-to-all-start = ((f32[128,8,512]{2,0,1:T(8,128)}), f32[128,8,512]{2,0,1:T(8,128)S(1)}, u32[]{:S(2)}, u32[]{:S(2)}) async-start(f32[128,8,512]{2,0,1:T(8,128)} %bitcast.155), calls=%async_computation | async-start | bytes 4194304 | tf_op jit(solution)/shard_map/all_to_all | solution.py:180
  183.3 69.8 %all-gather.9.cloned.1.call-start = ((), (), s32[]{:S(2)}) async-start(), calls=%async_computation.5 | async-start | bytes 1179648 | tf_op jit(solution)/shard_map/all_gather | solution.py:182
  218.5 36.6 %copy-start.8 = (f32[512]{0:T(512)S(1)}, f32[512]{0:T(512)}, u32[]{:S(2)}) copy-start(f32[512]{0:T(512)} %param.27) | copy-start | bytes 6148
Sparse Core Ops, SparseCore 0:
  62.3 30.6 all-gather.6
  96.1 22.0 all-gather.4
  160.4 55.9 reduce-scatter.1
  218.6 27.5 all-gather.8
